TPU v7x, 256 devices: a whole 4x4x8 slice. The times are simulated.
256 devices in a mesh: ctx: 32 (over z, x), head: 8 (over y, core).
Axes of the slice: x: 4, y: 4, z: 8, core: 2. Of those that a mesh axis runs over, the one named last changes fastest.
Arguments:
- queries: bfloat16 [16384, 4096], P('ctx', 'head'), may hold values from -6 to 6
- key_states: bfloat16 [16384, 512], P('ctx', 'head'), may hold values from -6 to 6
- value_states: bfloat16 [16384, 512], P('ctx', 'head'), may hold values from -6 to 6
- attn_out: bfloat16 [16384, 4096], P('ctx', 'head'), may hold values from -2 to 2
- grad_out: bfloat16 [16384, 4096], P('ctx', 'head'), may hold values from -6 to 6
- log_norm: float32 [32, 16384], P('head', 'ctx'), as said below
- doc_lengths: int32 [64], replicated, may hold values from 1 to 2048, as said below
Outputs:
- grad_queries: bfloat16 [16384, 4096], P('ctx', 'head')
- grad_keys: bfloat16 [16384, 512], P('ctx', 'head')
- grad_values: bfloat16 [16384, 512], P('ctx', 'head')
Inputs may be any that keep to these rules, and one draw needn't show every extreme that they name: `doc_lengths`: 64 document lengths that add up to 16384; one document has exactly 2048 tokens. `log_norm`: a given input, not recomputed from the others.
All inputs are finite; a program needn't handle non-finite values.
Results may differ from a plain program's by a relative error of at most 0.0051.
Values may be sent and summed in bfloat16 or wider, within the bound.
A program may use at most 64 MiB of HBM per device.

v0:
```python
import jax
import jax.numpy as jnp
from jax import lax
from jax.sharding import PartitionSpec as P

SPAN = 4


def partner(value, axis, apart):
    mask = 2**apart
    pairs = [(source, source ^ mask) for source in range(lax.axis_size(axis))]
    return lax.ppermute(value, axis, pairs)


def passed_along(value, axis, by):
    count = lax.axis_size(axis)
    pairs = [(i, i + by) for i in range(count) if 0 <= i + by < count]
    return lax.ppermute(value, axis, pairs)


def split_halves(stacked, head_size, upper_half):
    half_size = head_size // 2
    lower = jnp.concatenate(
        [stacked[..., :half_size], stacked[..., head_size : head_size + half_size]], axis=-1
    )
    upper = jnp.concatenate(
        [stacked[..., half_size:head_size], stacked[..., head_size + half_size :]], axis=-1
    )
    kept_half = jnp.where(upper_half, upper, lower)
    sent_half = jnp.where(upper_half, lower, upper)
    return (kept_half, sent_half)


def row_bounds(doc_lengths, shard_index, tok_rows):
    doc_ends = jnp.cumsum(doc_lengths)
    positions = shard_index * tok_rows + jnp.arange(tok_rows, dtype=jnp.int32)
    starts = jnp.sum(
        jnp.where(doc_ends[None, :] <= positions[:, None], doc_lengths[None, :], 0), axis=1
    )
    return (positions, starts)


def shard_pair(
    query_heads,
    grad_heads,
    norms,
    deltas,
    positions,
    starts,
    shard_keys,
    shard_values,
    first_key,
    score_scale,
):
    tok_rows = query_heads.shape[0]
    head_count = query_heads.shape[1]
    head_size = query_heads.shape[2]
    tile_rows = min(512, tok_rows)
    block_total = tok_rows // tile_rows
    gradients = jnp.zeros((tok_rows, 2 * head_size), jnp.float32)
    lowest_start = jnp.min(starts)
    highest_pos = positions[-1]

    def one_tile(key_block, carried):
        key_start = key_block * tile_rows
        lowest_key = first_key + key_start
        needed = (lowest_key <= highest_pos) & (lowest_key + tile_rows - 1 >= lowest_start)

        def compute_tile(state):
            query_grad, kv_grads = state
            key_pos = lowest_key + jnp.arange(tile_rows, dtype=jnp.int32)
            allowed = (key_pos[None, :] <= positions[:, None]) & (
                key_pos[None, :] >= starts[:, None]
            )
            scores = (
                jnp.einsum(
                    "qhd,kd->hqk", query_heads, shard_keys, preferred_element_type=jnp.float32
                )
                * score_scale
            )
            probs = jnp.where(allowed[None], jnp.exp(scores - norms[:, :, None]), jnp.float32(0.0))
            dprobs = jnp.einsum(
                "qhd,kd->hqk", grad_heads, shard_values, preferred_element_type=jnp.float32
            )
            dscores = probs * (dprobs - deltas[:, :, None])
            probs_b = probs.astype(jnp.bfloat16)
            dscores_b = dscores.astype(jnp.bfloat16)
            value_part = jnp.einsum(
                "hqk,qhd->kd", probs_b, grad_heads, preferred_element_type=jnp.float32
            )
            key_part = jnp.einsum(
                "hqk,qhd->kd", dscores_b, query_heads, preferred_element_type=jnp.float32
            )
            query_part = jnp.einsum(
                "hqk,kd->qhd", dscores_b, shard_keys, preferred_element_type=jnp.float32
            )
            previous = kv_grads
            kv_grads = previous + jnp.concatenate([key_part, value_part], 1)
            return (query_grad + query_part, kv_grads)

        return lax.cond(needed, compute_tile, lambda state: state, carried)

    start_state = (jnp.zeros((tile_rows, head_count, head_size), jnp.float32), gradients)
    query_grad, gradients = lax.fori_loop(0, block_total, one_tile, start_state)
    return (query_grad, gradients)


def local(queries, key_states, value_states, attn_out, grad_out, log_norm, doc_lengths):
    tok_rows = queries.shape[0]
    head_size = 2 * key_states.shape[1]
    head_count = queries.shape[1] // head_size
    score_scale = head_size ** (-0.5)
    ctx_index = lax.axis_index("ctx")
    upper_half = lax.axis_index("head") % 2 == 1
    other_keys, other_values = partner((key_states, value_states), "head", 0)
    full_keys = jnp.where(
        upper_half,
        jnp.concatenate([other_keys, key_states], 1),
        jnp.concatenate([key_states, other_keys], 1),
    )
    full_values = jnp.where(
        upper_half,
        jnp.concatenate([other_values, value_states], 1),
        jnp.concatenate([value_states, other_values], 1),
    )
    local_pair = jnp.concatenate([full_keys, full_values], axis=1)
    positions, starts = row_bounds(doc_lengths, ctx_index, tok_rows)
    row_delta = jnp.sum(
        (attn_out.astype(jnp.float32) * grad_out.astype(jnp.float32)).reshape(
            tok_rows, head_count, head_size
        ),
        axis=-1,
    )
    row_delta = jnp.transpose(row_delta)
    query_heads = queries.reshape(tok_rows, head_count, head_size)
    grad_heads = grad_out.reshape(tok_rows, head_count, head_size)

    def owner_pair(kv_block, distance):
        return shard_pair(
            query_heads,
            grad_heads,
            log_norm,
            row_delta,
            positions,
            starts,
            kv_block[:, :head_size],
            kv_block[:, head_size:],
            (ctx_index - distance) * tok_rows,
            score_scale,
        )

    query_total, own_terms = owner_pair(local_pair, 0)
    partials = [own_terms]
    for distance in range(1, SPAN + 1):
        arrived = passed_along(local_pair, "ctx", distance)
        query_part, kv_terms = owner_pair(arrived, distance)
        query_total = query_total + query_part
        partials.append(kv_terms)
    grad_queries = (
        (query_total * score_scale).reshape(tok_rows, head_count * head_size).astype(jnp.bfloat16)
    )
    summed = partials[0]
    for distance in range(1, SPAN + 1):
        summed = summed + passed_along(partials[distance], "ctx", -distance)
    kept_half, sent_half = split_halves(summed, head_size, upper_half)
    received = partner(sent_half, "head", 0)
    summed = kept_half + received
    half_size = head_size // 2
    grad_keys = (summed[:, :half_size] * score_scale).astype(jnp.bfloat16)
    grad_values = summed[:, half_size:].astype(jnp.bfloat16)
    return (grad_queries, grad_keys, grad_values)


def solution(mesh):
    in_specs = (
        P("ctx", "head"),
        P("ctx", "head"),
        P("ctx", "head"),
        P("ctx", "head"),
        P("ctx", "head"),
        P("head", "ctx"),
        P(),
    )
    out_specs = (P("ctx", "head"), P("ctx", "head"), P("ctx", "head"))
    return jax.shard_map(local, mesh=mesh, in_specs=in_specs, out_specs=out_specs, check_vma=False)
```

profile of v0, /device:TPU:41, one launch (start us, length us, event | category | flops | bytes accessed | tf_op | source)
XLA Modules:
  0.0 121.7 jit_solution(2094828855962129109)
XLA Ops:
  11.2 2.0 %copy.147 = bf16[512,512]{0,1:T(8,128)(2,1)} copy(bf16[512,512]{1,0:T(8,128)(2,1)} %param.21) | data formatting | bytes 1048576 | tf_op args[4]
  15.9 3.5 %collective-permute-start.5 = (bf16[512,256]{0,1:T(8,128)(2,1)}, bf16[512,256]{0,1:T(8,128)(2,1)}, u32[]{:S(2)}, u32[]{:S(2)}) collective-permute-start(bf16[512,256]{0,1:T(8,128)(2,1)} %pad_maximum_fusion), channel_id=1, source_target_pairs={{0,32},{8,40},{16,48},{24,56},{32,64},{40,72},{48,80},{56,88},{64,... | collective-permute-start | bytes 786440 | tf_op jit(solution)/shard_map/ppermute | solution.py:18
  19.4 4.4 %collective-permute-start.4 = (bf16[512,256]{0,1:T(8,128)(2,1)}, bf16[512,256]{0,1:T(8,128)(2,1)}, u32[]{:S(2)}, u32[]{:S(2)}) collective-permute-start(bf16[512,256]{0,1:T(8,128)(2,1)} %pad_maximum_fusion), channel_id=1, source_target_pairs={{0,24},{8,32},{16,40},{24,48},{32,56},{40,64},{48,72},{56,80},{64,... | collective-permute-start | bytes 786440 | tf_op jit(solution)/shard_map/ppermute | solution.py:18
  23.8 3.8 %collective-permute-start.3 = (bf16[512,256]{0,1:T(8,128)(2,1)}, bf16[512,256]{0,1:T(8,128)(2,1)}, u32[]{:S(2)}, u32[]{:S(2)}) collective-permute-start(bf16[512,256]{0,1:T(8,128)(2,1)} %pad_maximum_fusion), channel_id=1, source_target_pairs={{0,16},{8,24},{16,32},{24,40},{32,48},{40,56},{48,64},{56,72},{64,... | collective-permute-start | bytes 786440 | tf_op jit(solution)/shard_map/ppermute | solution.py:18
  27.6 2.5 %collective-permute-start.2 = (bf16[512,256]{0,1:T(8,128)(2,1)}, bf16[512,256]{0,1:T(8,128)(2,1)}, u32[]{:S(2)}, u32[]{:S(2)}) collective-permute-start(bf16[512,256]{0,1:T(8,128)(2,1)} %pad_maximum_fusion), channel_id=1, source_target_pairs={{0,8},{8,16},{16,24},{24,32},{32,40},{40,48},{48,56},{56,64},{64,7... | collective-permute-start | bytes 786440 | tf_op jit(solution)/shard_map/ppermute | solution.py:18
  32.6 12.3 %collective-permute-done.2 = bf16[512,256]{0,1:T(8,128)(2,1)} collective-permute-done((bf16[512,256]{0,1:T(8,128)(2,1)}, bf16[512,256]{0,1:T(8,128)(2,1)}, u32[]{:S(2)}, u32[]{:S(2)}) %collective-permute-start.2) | collective-permute-done | bytes 262176 | tf_op jit(solution)/shard_map/ppermute | solution.py:18
  44.9 8.2 %conditional.6 = (f32[512,4,128]{2,0,1:T(8,128)S(1)}, f32[512,256]{0,1:T(8,128)}) conditional(s32[]{:T(128)} %convert_element_type.69, (f32[512,4,128]{2,0,1:T(8,128)S(1)}, f32[512,256]{0,1:T(8,128)S(1)}) %tuple.53, (s32[]{:T(128)}, s32[512]{0:T(512)S(1)}, s32[512]{0:T(512)S(1)}, bf16[512,256]{0,1:T(8,128)(2,1)}, bf16[512,4,128]{0,2,1:T(8,128)(2,1)S(1)}, ...), branch_computations={%region_6.7_spmd, %region_7.8_spmd} | conditional | flops 1353974272 | bytes 30097512 | solution.py:101
  48.2 1.5 %fusion.19 = bf16[4,512,512]{1,2,0:T(8,128)(2,1)S(1)} fusion(f32[512,512,4]{1,0,2:T(8,128)S(1)} %fusion.30, bf16[512,4,128]{0,2,1:T(8,128)(2,1)S(1)} %copy-done.4, f32[4,512]{1,0:T(4,128)S(1)} %copy.152, f32[4,512]{1,0:T(4,128)S(1)} %copy-done.18, pred[512,512]{0,1:T(8,128)(4,1)S(1)} %compare_and_fusion.1, bf16[512,256]{1,0:T(8,128)(2,1)S(1)} %copy.151), kind=kOutput, calls=%fused_computation.24 | convolution fusion | flops 274726912 | bytes 7225344 | tf_op jit(solution)/shard_map/while/body/eval_jaxpr/cond/branch_1_fun/qhd,kd->hqk/dot_general | solution.py:82
  50.5 1.7 %fusion.26 = f32[512,4,128]{2,0,1:T(8,128)S(1)} fusion(f32[512,4,128]{2,0,1:T(8,128)S(1)} %get-tuple-element.286, bf16[4,512,512]{1,2,0:T(8,128)(2,1)S(1)} %fusion.19, bf16[512,256]{1,0:T(8,128)(2,1)} %copy-done), kind=kOutput, calls=%fused_computation.32 | convolution fusion | flops 268697600 | bytes 4325376 | tf_op jit(solution)/shard_map/while/body/eval_jaxpr/cond/branch_1_fun/hqk,kd->qhd/dot_general | solution.py:94
  53.1 1.9 %collective-permute-start.6 = (f32[512,256]{0,1:T(8,128)}, f32[512,256]{0,1:T(8,128)}, u32[]{:S(2)}, u32[]{:S(2)}) collective-permute-start(f32[512,256]{0,1:T(8,128)} %get-tuple-element.414), channel_id=1, source_target_pairs={{8,0},{16,8},{24,16},{32,24},{40,32},{48,40},{56,48},{64,56},{72,6... | collective-permute-start | bytes 1572872 | tf_op jit(solution)/shard_map/ppermute | solution.py:18
  55.0 1.8 %conditional.7 = (f32[512,4,128]{2,0,1:T(8,128)}, f32[512,256]{0,1:T(8,128)}) conditional(s32[]{:T(128)} %convert_element_type.70, (f32[512,4,128]{2,0,1:T(8,128)S(1)}, f32[512,256]{0,1:T(8,128)S(1)}) %tuple.53, (s32[]{:T(128)}, s32[512]{0:T(512)S(1)}, s32[512]{0:T(512)S(1)}, bf16[512,256]{0,1:T(8,128)(2,1)}, bf16[512,4,128]{0,2,1:T(8,128)(2,1)S(1)}, ...), branch_computations={%region_8.9_spmd, %region_9.10_spmd} | conditional | flops 1353974272 | bytes 31178912 | solution.py:101
  56.9 1.9 %collective-permute-start.7 = (f32[512,256]{0,1:T(8,128)}, f32[512,256]{0,1:T(8,128)}, u32[]{:S(2)}, u32[]{:S(2)}) collective-permute-start(f32[512,256]{0,1:T(8,128)} %get-tuple-element.430), channel_id=1, source_target_pairs={{16,0},{24,8},{32,16},{40,24},{48,32},{56,40},{64,48},{72,56},{80,... | collective-permute-start | bytes 1572872 | tf_op jit(solution)/shard_map/ppermute | solution.py:18
  58.8 1.8 %conditional.8 = (f32[512,4,128]{2,0,1:T(8,128)}, f32[512,256]{0,1:T(8,128)}) conditional(s32[]{:T(128)} %convert_element_type.71, (f32[512,4,128]{2,0,1:T(8,128)S(1)}, f32[512,256]{0,1:T(8,128)S(1)}) %tuple.53, (s32[]{:T(128)}, s32[512]{0:T(512)S(1)}, s32[512]{0:T(512)S(1)}, bf16[512,256]{0,1:T(8,128)(2,1)}, bf16[512,4,128]{0,2,1:T(8,128)(2,1)S(1)}, ...), branch_computations={%region_10.11_spmd, %region_11.12_spmd} | conditional | flops 1353974272 | bytes 31178912 | solution.py:101
  60.6 1.9 %collective-permute-start.8 = (f32[512,256]{0,1:T(8,128)}, f32[512,256]{0,1:T(8,128)}, u32[]{:S(2)}, u32[]{:S(2)}) collective-permute-start(f32[512,256]{0,1:T(8,128)} %get-tuple-element.431), channel_id=1, source_target_pairs={{24,0},{32,8},{40,16},{48,24},{56,32},{64,40},{72,48},{80,56},{88,... | collective-permute-start | bytes 1572872 | tf_op jit(solution)/shard_map/ppermute | solution.py:18
  62.5 1.8 %conditional.9 = (f32[512,4,128]{2,0,1:T(8,128)}, f32[512,256]{0,1:T(8,128)}) conditional(s32[]{:T(128)} %convert_element_type.72, (f32[512,4,128]{2,0,1:T(8,128)S(1)}, f32[512,256]{0,1:T(8,128)S(1)}) %tuple.53, (s32[]{:T(128)}, s32[512]{0:T(512)S(1)}, s32[512]{0:T(512)S(1)}, bf16[512,256]{0,1:T(8,128)(2,1)}, bf16[512,4,128]{0,2,1:T(8,128)(2,1)S(1)}, ...), branch_computations={%region_12.13_spmd, %region_13.14_spmd} | conditional | flops 1353974272 | bytes 31178912 | solution.py:101
  64.3 1.9 %collective-permute-start.9 = (f32[512,256]{0,1:T(8,128)}, f32[512,256]{0,1:T(8,128)}, u32[]{:S(2)}, u32[]{:S(2)}) collective-permute-start(f32[512,256]{0,1:T(8,128)} %get-tuple-element.432), channel_id=1, source_target_pairs={{32,0},{40,8},{48,16},{56,24},{64,32},{72,40},{80,48},{88,56},{96,... | collective-permute-start | bytes 1572872 | tf_op jit(solution)/shard_map/ppermute | solution.py:18
  67.6 6.3 %conditional.5 = ((f32[512,4,128]{2,0,1:T(8,128)S(1)}, f32[512,256]{0,1:T(8,128)S(1)})) conditional(s32[]{:T(128)} %convert_element_type.66, (f32[512,4,128]{2,0,1:T(8,128)S(1)}, f32[512,256]{0,1:T(8,128)S(1)}) %tuple.53, (s32[]{:T(128)}, s32[512]{0:T(512)S(1)}, s32[512]{0:T(512)S(1)}, bf16[512,128]{0,1:T(8,128)(2,1)S(1)}, ...), branch_computations={%region_4.5_spmd, %region_5.6_spmd} | conditional | flops 1353974272 | bytes 29081740 | solution.py:101
  70.5 1.6 %fusion.1 = bf16[4,512,512]{1,2,0:T(8,128)(2,1)S(1)} fusion(f32[512,512,4]{1,0,2:T(8,128)S(1)} %fusion.13, bf16[512,4,128]{0,2,1:T(8,128)(2,1)S(1)} %copy-done.8, f32[4,512]{1,0:T(4,128)S(1)} %copy-done.17, f32[4,512]{1,0:T(4,128)S(1)} %copy-done.22, pred[512,512]{0,1:T(8,128)(4,1)S(1)} %compare_and_fusion, bf16[512,128]{0,1:T(8,128)(2,1)S(1)} %copy-done.10), kind=kOutput, calls=%fused_computation.2 | convolution fusion | flops 274726912 | bytes 7225344 | tf_op jit(solution)/shard_map/while/body/eval_jaxpr/cond/branch_1_fun/qhd,kd->hqk/dot_general | solution.py:82
  73.9 10.4 %collective-permute-done.7 = f32[512,256]{0,1:T(8,128)} collective-permute-done((f32[512,256]{0,1:T(8,128)}, f32[512,256]{0,1:T(8,128)}, u32[]{:S(2)}, u32[]{:S(2)}) %collective-permute-start.7) | collective-permute-done | bytes 524320 | tf_op jit(solution)/shard_map/ppermute | solution.py:18
  84.3 12.0 %collective-permute-done.8 = f32[512,256]{0,1:T(8,128)} collective-permute-done((f32[512,256]{0,1:T(8,128)}, f32[512,256]{0,1:T(8,128)}, u32[]{:S(2)}, u32[]{:S(2)}) %collective-permute-start.8) | collective-permute-done | bytes 524320 | tf_op jit(solution)/shard_map/ppermute | solution.py:18
  96.3 17.9 %collective-permute-done.9 = f32[512,256]{0,1:T(8,128)} collective-permute-done((f32[512,256]{0,1:T(8,128)}, f32[512,256]{0,1:T(8,128)}, u32[]{:S(2)}, u32[]{:S(2)}) %collective-permute-start.9) | collective-permute-done | bytes 524320 | tf_op jit(solution)/shard_map/ppermute | solution.py:18
  114.2 1.8 %add_add_fusion = f32[512,256]{0,1:T(8,128)S(1)} fusion(f32[512,256]{0,1:T(8,128)} %collective-permute-done.9, f32[512,256]{0,1:T(8,128)} %collective-permute-done.8, f32[512,256]{0,1:T(8,128)} %collective-permute-done.7, f32[512,256]{0,1:T(8,128)S(1)} %get-tuple-element.413, f32[512,256]{0,1:T(8,128)} %collective-permute-done.6), kind=kLoop, calls=%fused_computation.110 | loop fusion | flops 524288 | bytes 3145728 | tf_op jit(solution)/shard_map/add | solution.py:164
  116.1 1.4 %collective-permute-start.10 = (f32[512,128]{0,1:T(8,128)S(1)}, f32[512,128]{0,1:T(8,128)S(1)}, u32[]{:S(2)}, u32[]{:S(2)}) collective-permute-start(f32[512,128]{0,1:T(8,128)S(1)} %fusion.79), channel_id=1, source_target_pairs={{0,1},{1,0},{2,3},{3,2},{4,5},{5,4},{6,7},{7,6},{8,9},{9,8},{10,11... | collective-permute-start | bytes 786440 | tf_op jit(solution)/shard_map/ppermute | solution.py:12
  117.5 2.9 %copy_bitcast_fusion = bf16[512,512]{1,0:T(8,128)(2,1)} fusion(f32[512,4,128]{2,0,1:T(8,128)} %get-tuple-element.412, f32[512,4,128]{2,0,1:T(8,128)} %get-tuple-element.411, f32[512,4,128]{2,0,1:T(8,128)} %get-tuple-element.410, f32[512,4,128]{2,0,1:T(8,128)S(1)} %get-tuple-element.408, f32[512,4,128]{2,0,1:T(8,128)S(1)} %get-tuple-element.409), kind=kLoop, calls=%fused_computation.109 | loop fusion | flops 1572864 | bytes 5767168 | tf_op jit(solution)/shard_map/convert_element_type | solution.py:160
  (68 shorter events, 26.7 us)
Async XLA Ops:
  0.6 12.6 %collective-permute-start = (bf16[512,64]{0,1:T(8,128)(2,1)}, bf16[512,64]{0,1:T(8,128)(2,1)S(1)}, u32[]{:S(2)}, u32[]{:S(2)}) collective-permute-start(bf16[512,64]{0,1:T(8,128)(2,1)} %param.18), channel_id=1, source_target_pairs={{0,1},{1,0},{2,3},{3,2},{4,5},{5,4},{6,7},{7,6},{8,9},{9,8},{10,11... | collective-permute-start | bytes 196616 | tf_op jit(solution)/shard_map/ppermute | solution.py:12
  1.4 12.8 %collective-permute-start.1 = (bf16[512,64]{0,1:T(8,128)(2,1)}, bf16[512,64]{0,1:T(8,128)(2,1)S(1)}, u32[]{:S(2)}, u32[]{:S(2)}) collective-permute-start(bf16[512,64]{0,1:T(8,128)(2,1)} %param.19), channel_id=1, source_target_pairs={{0,1},{1,0},{2,3},{3,2},{4,5},{5,4},{6,7},{7,6},{8,9},{9,8},{10,11... | collective-permute-start | bytes 196616 | tf_op jit(solution)/shard_map/ppermute | solution.py:12
  15.1 16.7 %copy-start.9 = (bf16[512,128]{0,1:T(8,128)(2,1)}, bf16[512,128]{0,1:T(8,128)(2,1)S(1)}, u32[]{:S(2)}) copy-start(bf16[512,128]{0,1:T(8,128)(2,1)S(1)} %maximum_select_fusion.1) | copy-start | bytes 393220
  15.9 46.6 %collective-permute-start.5 = (bf16[512,256]{0,1:T(8,128)(2,1)}, bf16[512,256]{0,1:T(8,128)(2,1)}, u32[]{:S(2)}, u32[]{:S(2)}) collective-permute-start(bf16[512,256]{0,1:T(8,128)(2,1)} %pad_maximum_fusion), channel_id=1, source_target_pairs={{0,32},{8,40},{16,48},{24,56},{32,64},{40,72},{48,80},{56,88},{64,... | collective-permute-start | bytes 786440 | tf_op jit(solution)/shard_map/ppermute | solution.py:18
  19.4 39.4 %collective-permute-start.4 = (bf16[512,256]{0,1:T(8,128)(2,1)}, bf16[512,256]{0,1:T(8,128)(2,1)}, u32[]{:S(2)}, u32[]{:S(2)}) collective-permute-start(bf16[512,256]{0,1:T(8,128)(2,1)} %pad_maximum_fusion), channel_id=1, source_target_pairs={{0,24},{8,32},{16,40},{24,48},{32,56},{40,64},{48,72},{56,80},{64,... | collective-permute-start | bytes 786440 | tf_op jit(solution)/shard_map/ppermute | solution.py:18
  23.8 31.2 %collective-permute-start.3 = (bf16[512,256]{0,1:T(8,128)(2,1)}, bf16[512,256]{0,1:T(8,128)(2,1)}, u32[]{:S(2)}, u32[]{:S(2)}) collective-permute-start(bf16[512,256]{0,1:T(8,128)(2,1)} %pad_maximum_fusion), channel_id=1, source_target_pairs={{0,16},{8,24},{16,32},{24,40},{32,48},{40,56},{48,64},{56,72},{64,... | collective-permute-start | bytes 786440 | tf_op jit(solution)/shard_map/ppermute | solution.py:18
  27.6 17.3 %collective-permute-start.2 = (bf16[512,256]{0,1:T(8,128)(2,1)}, bf16[512,256]{0,1:T(8,128)(2,1)}, u32[]{:S(2)}, u32[]{:S(2)}) collective-permute-start(bf16[512,256]{0,1:T(8,128)(2,1)} %pad_maximum_fusion), channel_id=1, source_target_pairs={{0,8},{8,16},{16,24},{24,32},{32,40},{40,48},{48,56},{56,64},{64,7... | collective-permute-start | bytes 786440 | tf_op jit(solution)/shard_map/ppermute | solution.py:18
  44.9 2.2 %copy-start.4 = (bf16[512,4,128]{0,2,1:T(8,128)(2,1)S(1)}, bf16[512,4,128]{0,2,1:T(8,128)(2,1)}, u32[]{:S(2)}) copy-start(bf16[512,4,128]{0,2,1:T(8,128)(2,1)} %get-tuple-element.319) | copy-start | bytes 1572868 | tf_op jit(solution)/shard_map/while/body/eval_jaxpr/cond
  46.4 1.8 %copy-start = (bf16[512,256]{1,0:T(8,128)(2,1)}, bf16[512,256]{1,0:T(8,128)(2,1)S(1)}, u32[]{:S(2)}) copy-start(bf16[512,256]{1,0:T(8,128)(2,1)S(1)} %copy.151) | copy-start | bytes 786436 | tf_op jit(solution)/shard_map/while/body/eval_jaxpr/cond
  46.4 0.7 copy-start.18
  53.1 20.8 %collective-permute-start.6 = (f32[512,256]{0,1:T(8,128)}, f32[512,256]{0,1:T(8,128)}, u32[]{:S(2)}, u32[]{:S(2)}) collective-permute-start(f32[512,256]{0,1:T(8,128)} %get-tuple-element.414), channel_id=1, source_target_pairs={{8,0},{16,8},{24,16},{32,24},{40,32},{48,40},{56,48},{64,56},{72,6... | collective-permute-start | bytes 1572872 | tf_op jit(solution)/shard_map/ppermute | solution.py:18
  56.9 27.4 %collective-permute-start.7 = (f32[512,256]{0,1:T(8,128)}, f32[512,256]{0,1:T(8,128)}, u32[]{:S(2)}, u32[]{:S(2)}) collective-permute-start(f32[512,256]{0,1:T(8,128)} %get-tuple-element.430), channel_id=1, source_target_pairs={{16,0},{24,8},{32,16},{40,24},{48,32},{56,40},{64,48},{72,56},{80,... | collective-permute-start | bytes 1572872 | tf_op jit(solution)/shard_map/ppermute | solution.py:18
  60.6 35.7 %collective-permute-start.8 = (f32[512,256]{0,1:T(8,128)}, f32[512,256]{0,1:T(8,128)}, u32[]{:S(2)}, u32[]{:S(2)}) collective-permute-start(f32[512,256]{0,1:T(8,128)} %get-tuple-element.431), channel_id=1, source_target_pairs={{24,0},{32,8},{40,16},{48,24},{56,32},{64,40},{72,48},{80,56},{88,... | collective-permute-start | bytes 1572872 | tf_op jit(solution)/shard_map/ppermute | solution.py:18
  64.3 49.9 %collective-permute-start.9 = (f32[512,256]{0,1:T(8,128)}, f32[512,256]{0,1:T(8,128)}, u32[]{:S(2)}, u32[]{:S(2)}) collective-permute-start(f32[512,256]{0,1:T(8,128)} %get-tuple-element.432), channel_id=1, source_target_pairs={{32,0},{40,8},{48,16},{56,24},{64,32},{72,40},{80,48},{88,56},{96,... | collective-permute-start | bytes 1572872 | tf_op jit(solution)/shard_map/ppermute | solution.py:18
  68.3 1.0 copy-start.8
  68.3 1.0 copy-start.22
  69.4 1.1 copy-start.10
  69.4 1.1 copy-start.17
  116.1 4.3 %collective-permute-start.10 = (f32[512,128]{0,1:T(8,128)S(1)}, f32[512,128]{0,1:T(8,128)S(1)}, u32[]{:S(2)}, u32[]{:S(2)}) collective-permute-start(f32[512,128]{0,1:T(8,128)S(1)} %fusion.79), channel_id=1, source_target_pairs={{0,1},{1,0},{2,3},{3,2},{4,5},{5,4},{6,7},{7,6},{8,9},{9,8},{10,11... | collective-permute-start | bytes 786440 | tf_op jit(solution)/shard_map/ppermute | solution.py:12
where the time goes:
time: 123 us; the launch traced here: 122 us
  waiting for transfers between devices  52.6 us (43%)
  starting transfers between devices  24.1 us (20%)
  other arithmetic  13.2 us (11%)
  local copies, waits for them, and re-layouts  13.2 us (11%)
  matrix products  10.8 us (9%)
  between operations  7.52 us (6%)
    ppermute x8, waiting for transfers between devices, passed_along(): return lax.ppermute(value, axis, pairs)  52.6 us
    ppermute x8, starting transfers between devices, passed_along(): return lax.ppermute(value, axis, pairs)  21.9 us
    cond x20, local copies, waits for them, and re-layouts  5.45 us
    unnamed x4, local copies, waits for them, and re-layouts  3.31 us
    dot_general x2, matrix products, compute_tile(): jnp.einsum('qhd,kd->hqk', grad_heads, shard_values, preferred_element_typ...  3.08 us
    convert_element_type x1, other arithmetic, local(): (query_total * score_scale).reshape(tok_rows, head_count * head_size)  2.88 us
    another operation x6, local copies, waits for them, and re-layouts  2.77 us
    dot_general x2, matrix products, compute_tile(): jnp.einsum('hqk,kd->qhd', dscores_b, shard_keys, preferred_element_type=j...  2.59 us
  transfers between devices with their start and end apart: 11, of which 4 were waited for; matrix products, arithmetic and copies ran while one was open for 27% of the time, Pallas kernels for 0%

commit v1 on v0

v1 whole, which is shorter than its diff:
```python
import functools

import jax
import jax.numpy as jnp
from jax import lax
from jax.experimental import pallas as pl
from jax.experimental.pallas import tpu as pltpu
from jax.sharding import PartitionSpec as P

MESH = pl.DeviceIdType.MESH
LOG2E = 1.4426950408889634
NT = (((1,), (1,)), ((), ()))
NN = (((1,), (0,)), ((), ()))
SPAN = 4
ORDER = (0, 1, 3, 2, 4)


def mm(a, b, dims):
    return lax.dot_general(a, b, dims, preferred_element_type=jnp.float32)


def kernel(
    doc_ref, q_hbm, k_hbm, v_hbm, o_hbm, do_hbm, ln_hbm,
    dq_hbm, dk_hbm, dv_hbm,
    q, o, do, ln, qt, dot, dl, st, hb, kn, vn, kt, g, pr, sb, rb, dqt, dq, dk, dv,
    in_sem, out_sem, hs_sem, hr_sem, ps_sem, pr_sem, gs_sem, gr_sem, is_sem, ir_sem,
):
    rows, heads = q.shape[0], qt.shape[0]
    dim = q.shape[1] // heads
    half = dim // 2
    mid = rows // 2
    n_ctx = lax.axis_size("ctx")
    scale = dim ** (-0.5)
    me = lax.axis_index("ctx")
    head = lax.axis_index("head")
    core = lax.rem(head, 2)
    pair = head + 1 - 2 * core

    def at(shift):
        return lax.rem(me + shift + n_ctx, n_ctx)

    loads = [
        pltpu.make_async_copy(src, dst, in_sem.at[n])
        for n, (src, dst) in enumerate(
            (
                (k_hbm, hb.at[0, core, 0:half]), (v_hbm, hb.at[0, core, half:dim]),
                (q_hbm, q), (do_hbm, do), (o_hbm, o), (ln_hbm, ln),
            )
        )
    ]
    for c in loads:
        c.start()

    barrier = pltpu.get_barrier_semaphore()
    pl.semaphore_signal(barrier, inc=1, device_id=(me, pair), device_id_type=MESH)
    for d in range(1, SPAN + 1):
        pl.semaphore_signal(barrier, inc=1, device_id=(at(d), head), device_id_type=MESH)
        pl.semaphore_signal(barrier, inc=1, device_id=(at(-d), head), device_id_type=MESH)

    pos = me * rows + lax.broadcasted_iota(jnp.int32, (1, rows), 1)

    def one_doc(j, carry):
        end, start = carry
        end = end + doc_ref[j]
        return end, jnp.where(pos >= end, end, start)

    _, start = lax.fori_loop(
        0, doc_ref.shape[0], one_doc, (jnp.int32(0), jnp.zeros((1, rows), jnp.int32))
    )
    st[...] = start

    for c in loads:
        c.wait()
    for h in range(heads):
        cols = slice(h * dim, (h + 1) * dim)
        qt[h] = q[:, cols].T
        dot[h] = do[:, cols].T
        dl[h : h + 1, :] = jnp.sum(
            dot[h].astype(jnp.float32) * o[:, cols].T.astype(jnp.float32), axis=0, keepdims=True
        )
    ln[...] = ln[...] * LOG2E

    pl.semaphore_wait(barrier, 1 + 2 * SPAN)

    def to_pair(src, dst, send, recv):
        return pltpu.make_async_remote_copy(
            src, dst, send, recv, device_id=(me, pair), device_id_type=MESH
        )

    def fwd(d):
        return to_pair(hb.at[d, core], hb.at[d, core], ps_sem.at[d], pr_sem.at[d])

    def ici(d):
        return pltpu.make_async_remote_copy(
            hb.at[0, core], hb.at[d, core], hs_sem.at[d - 1], hr_sem.at[d - 1],
            device_id=(at(d), head), device_id_type=MESH,
        )

    def gpair(d):
        return to_pair(g.at[d, 1 - core], pr.at[d], gs_sem.at[d], gr_sem.at[d])

    def gici(d):
        return pltpu.make_async_remote_copy(
            sb.at[d - 1], rb.at[d - 1], is_sem.at[d - 1], ir_sem.at[d - 1],
            device_id=(at(-d), head), device_id_type=MESH,
        )

    fwd(0).start()
    for d in ORDER[1:]:
        ici(d).start()

    def one_head(d, h, first):
        cols = slice(h * dim, (h + 1) * dim)
        if d == 0:
            parts = ((0, mid, 0, rows), (mid, rows, mid, rows))
        elif d == SPAN:
            parts = ((0, mid, 0, mid), (mid, rows, 0, rows))
        else:
            parts = ((0, rows, 0, rows),)
        seen = set()
        for klo, khi, qlo, qhi in parts:
            size = (khi - klo, qhi - qlo)
            s = mm(kn[klo:khi, :], q[qlo:qhi, cols], NT)
            dp = mm(vn[klo:khi, :], do[qlo:qhi, cols], NT)
            kpos = (me - d) * rows + klo + lax.broadcasted_iota(jnp.int32, size, 0)
            allowed = kpos >= st[:, qlo:qhi]
            if d == 0:
                qpos = me * rows + qlo + lax.broadcasted_iota(jnp.int32, size, 1)
                allowed = allowed & (kpos <= qpos)
            p = jnp.where(
                allowed, jnp.exp2(s * (scale * LOG2E) - ln[h : h + 1, qlo:qhi]), 0.0
            )
            ds = p * (dp - dl[h : h + 1, qlo:qhi])
            pb = p.astype(jnp.bfloat16)
            dsb = ds.astype(jnp.bfloat16)
            gk = mm(qt[h, :, qlo:qhi], dsb, NT)
            gv = mm(dot[h, :, qlo:qhi], pb, NT)
            for c in range(2):
                part = jnp.concatenate(
                    [gk[c * half : (c + 1) * half], gv[c * half : (c + 1) * half]], axis=0
                )
                if h == 0:
                    g[d, c, :, klo:khi] = part
                else:
                    g[d, c, :, klo:khi] += part
            gq = mm(kt[:, klo:khi], dsb, NN)
            if first and not seen:
                dqt[h, :, qlo:qhi] = gq
            else:
                dqt[h, :, qlo:qhi] += gq
            seen.add(klo)

    for i, d in enumerate(ORDER):
        fwd(d).wait_recv()
        kt[...] = jnp.concatenate([hb[d, 0, :half], hb[d, 1, :half]], axis=0)
        kn[...] = kt[...].T
        vn[...] = jnp.concatenate([hb[d, 0, half:], hb[d, 1, half:]], axis=0).T
        for h in range(heads):
            if h == heads // 2:
                if i + 1 < len(ORDER):
                    nxt = ORDER[i + 1]
                    ici(nxt).wait_recv()
                    fwd(nxt).start()
                if i >= 1 and ORDER[i - 1] != 0:
                    prev = ORDER[i - 1]
                    gpair(prev).wait_recv()
                    sb[prev - 1] = (g[prev, core] + pr[prev]).astype(jnp.bfloat16)
            if h == heads // 2 + 1 and i >= 1 and ORDER[i - 1] != 0:
                gici(ORDER[i - 1]).start()
            one_head(d, h, i == 0)
        gpair(d).start()

    stores = [
        pltpu.make_async_copy(src, dst, out_sem.at[n])
        for n, (src, dst) in enumerate(((dq, dq_hbm), (dk, dk_hbm), (dv, dv_hbm)))
    ]
    last = ORDER[-1]
    for h in range(heads // 2):
        dq[:, h * dim : (h + 1) * dim] = (dqt[h].T * scale).astype(jnp.bfloat16)
    gpair(last).wait_recv()
    sb[last - 1] = (g[last, core] + pr[last]).astype(jnp.bfloat16)
    for h in range(heads // 2, heads):
        dq[:, h * dim : (h + 1) * dim] = (dqt[h].T * scale).astype(jnp.bfloat16)
    gici(last).start()
    stores[0].start()
    gpair(0).wait_recv()
    total = g[0, core] + pr[0]
    for d in ORDER[1:]:
        gici(d).wait_recv()
        total = total + rb[d - 1].astype(jnp.float32)
    dk[...] = (total[:half] * scale).astype(jnp.bfloat16)
    dv[...] = total[half:].astype(jnp.bfloat16)
    stores[1].start()
    stores[2].start()
    for d in range(SPAN + 1):
        fwd(d).wait_send()
        gpair(d).wait_send()
        if d:
            ici(d).wait_send()
            gici(d).wait_send()
    for c in stores:
        c.wait()


def local(queries, key_states, value_states, attn_out, grad_out, log_norm, doc_lengths):
    rows, half = key_states.shape
    dim = 2 * half
    heads = queries.shape[1] // dim
    bf, f32 = jnp.bfloat16, jnp.float32
    blocks = SPAN + 1
    anywhere = pl.BlockSpec(memory_space=pl.ANY)
    vmem, dma = pltpu.VMEM, pltpu.SemaphoreType.DMA
    grad_q, grad_k, grad_v = pl.pallas_call(
        kernel,
        out_shape=(
            jax.ShapeDtypeStruct((rows, heads * dim), bf),
            jax.ShapeDtypeStruct((half, rows), bf),
            jax.ShapeDtypeStruct((half, rows), bf),
        ),
        in_specs=[pl.BlockSpec(memory_space=pltpu.SMEM)] + [anywhere] * 6,
        out_specs=(anywhere,) * 3,
        scratch_shapes=[
            vmem((rows, heads * dim), bf),
            vmem((rows, heads * dim), bf),
            vmem((rows, heads * dim), bf),
            vmem((heads, rows), f32),
            vmem((heads, dim, rows), bf),
            vmem((heads, dim, rows), bf),
            vmem((heads, rows), f32),
            vmem((1, rows), jnp.int32),
            vmem((blocks, 2, dim, rows), bf),
            vmem((rows, dim), bf),
            vmem((rows, dim), bf),
            vmem((dim, rows), bf),
            vmem((blocks, 2, dim, rows), f32),
            vmem((blocks, dim, rows), f32),
            vmem((SPAN, dim, rows), bf),
            vmem((SPAN, dim, rows), bf),
            vmem((heads, dim, rows), f32),
            vmem((rows, heads * dim), bf),
            vmem((half, rows), bf),
            vmem((half, rows), bf),
            dma((6,)), dma((3,)),
            dma((SPAN,)), dma((SPAN,)), dma((blocks,)), dma((blocks,)),
            dma((blocks,)), dma((blocks,)), dma((SPAN,)), dma((SPAN,)),
        ],
        compiler_params=pltpu.CompilerParams(
            collective_id=0, has_side_effects=True, vmem_limit_bytes=60 * 2**20
        ),
    )(doc_lengths, queries, key_states.T, value_states.T, attn_out, grad_out, log_norm)
    return grad_q, grad_k.T, grad_v.T


def solution(mesh):
    in_specs = (
        P("ctx", "head"), P("ctx", "head"), P("ctx", "head"), P("ctx", "head"),
        P("ctx", "head"), P("head", "ctx"), P(),
    )
    out_specs = (P("ctx", "head"), P("ctx", "head"), P("ctx", "head"))
    return jax.shard_map(local, mesh=mesh, in_specs=in_specs, out_specs=out_specs, check_vma=False)
```

time: 123 us -> 43.5 us (0.35)
  the two profiles are of different devices: /device:TPU:41 before, /device:TPU:1 now
where the time goes in v1:
time: 43.5 us; the launch traced here: 43.3 us
  Pallas kernels  39.3 us (90%)
  local copies, waits for them, and re-layouts  3.4 us (8%)
  between operations  0.65 us (1%)
    pallas_call x1, Pallas kernels, local(): pl.pallas_call(kernel, out_shape=(jax.ShapeDtypeStruct((rows, heads * dim...  39.3 us
    unnamed x7, local copies, waits for them, and re-layouts  3.4 us

profile of v1, /device:TPU:1, one launch (start us, length us, event | category | flops | bytes accessed | tf_op | source)
XLA Modules:
  0.0 43.3 jit_solution(11655475833103815257)
XLA Ops:
  0.6 39.3 %shard_map.94 = (bf16[512,512]{1,0:T(8,128)(2,1)}, bf16[64,512]{1,0:T(8,128)(2,1)}, bf16[64,512]{1,0:T(8,128)(2,1)}) custom-call(s32[64]{0:T(128)} %doc_ref.1, bf16[512,512]{1,0:T(8,128)(2,1)} %q_hbm.1, bf16[64,512]{1,0:T(8,128)(2,1)} %bitcast.4, bf16[64,512]{1,0:T(8,128)(2,1)} %bitcast.5, bf16[512,512]{1,0:T(8,128)(2,1)} %o_hbm.1, bf16[512,512]{1,0:T(8,128)(2,1)} %do_hbm.1, ...), custom_call_target="tpu_custom_call" | custom-call | tf_op jit(solution)/shard_map/pallas_call | solution.py:213
  39.9 0.0 copy-start.1
  39.9 1.9 %copy.13 = bf16[512,512]{1,0:T(8,128)(2,1)} copy(bf16[512,512]{1,0:T(8,128)(2,1)} %get-tuple-element.12) | data formatting | bytes 1048576
  41.8 0.0 copy-done.1
  41.8 0.0 copy-start
  41.8 0.6 %copy.14 = bf16[512,64]{0,1:T(8,128)(2,1)} copy(bf16[512,64]{0,1:T(8,128)(2,1)S(1)} %bitcast.7) | data formatting | bytes 131072
  42.5 0.2 copy-done
  42.7 0.6 %copy.15 = bf16[512,64]{0,1:T(8,128)(2,1)} copy(bf16[512,64]{0,1:T(8,128)(2,1)S(1)} %bitcast.6) | data formatting | bytes 131072
Async XLA Ops:
  39.9 1.9 %copy-start.1 = (bf16[64,512]{1,0:T(8,128)(2,1)S(1)}, bf16[64,512]{1,0:T(8,128)(2,1)}, u32[]{:S(2)}) copy-start(bf16[64,512]{1,0:T(8,128)(2,1)} %get-tuple-element.7) | copy-start | bytes 196612
  41.8 0.9 %copy-start = (bf16[64,512]{1,0:T(8,128)(2,1)S(1)}, bf16[64,512]{1,0:T(8,128)(2,1)}, u32[]{:S(2)}) copy-start(bf16[64,512]{1,0:T(8,128)(2,1)} %get-tuple-element.8) | copy-start | bytes 196612

commit v2 on v1

v2 whole, which is shorter than its diff:
```python
import jax
import jax.numpy as jnp
from jax import lax
from jax.experimental import pallas as pl
from jax.experimental.pallas import tpu as pltpu
from jax.sharding import PartitionSpec as P

MESH = pl.DeviceIdType.MESH
LOG2E = 1.4426950408889634
NT = (((1,), (1,)), ((), ()))
NN = (((1,), (0,)), ((), ()))
SPAN = 4
GATHER = (4, 1, 2, 3)
BLOCKS = (1, 2, 3)
RETURN = (1, 2, 3, 4)


def mm(a, b, dims):
    return lax.dot_general(a, b, dims, preferred_element_type=jnp.float32)


def kernel(
    doc_ref, q_hbm, k_hbm, v_hbm, o_hbm, do_hbm, ln_hbm,
    dq_hbm, dk_hbm, dv_hbm,
    kv, q, do, o, qt, dot, ln, dl, st, hb, kn, vn, kt, g, r0, sb, rb, dqt, dqi, dq, dk, dv,
    in_sem, out_sem, ps_sem, pr_sem, hs_sem, hr_sem, gs_sem, gr_sem, qs_sem, qr_sem,
):
    part = q.shape[2]
    rows = 2 * part
    heads = qt.shape[1]
    dim = qt.shape[3]
    half = dim // 2
    n_ctx = lax.axis_size("ctx")
    scale = dim ** (-0.5)
    me = lax.axis_index("ctx")
    head = lax.axis_index("head")
    core = lax.rem(head, 2)
    base = head - core
    pair = base + 1 - core

    pieces = []
    for i in range(2):
        at = pl.ds(i * part, part)
        pieces += [
            (k_hbm.at[:, at], kv.at[i, 0:half]),
            (v_hbm.at[:, at], kv.at[i, half:dim]),
            (q_hbm.at[at], q.at[0, i]),
            (do_hbm.at[at], do.at[0, i]),
            (o_hbm.at[at], o.at[i]),
            (ln_hbm.at[:, at], ln.at[0, i]),
        ]
    loads = [pltpu.make_async_copy(s, d, in_sem.at[n]) for n, (s, d) in enumerate(pieces)]
    for c in loads:
        c.start()

    barrier = pltpu.get_barrier_semaphore()
    pl.semaphore_signal(barrier, inc=1, device_id=(me, pair), device_id_type=MESH)
    expected = jnp.int32(1)
    for d in range(1, SPAN + 1):

        @pl.when(me >= d)
        def _():
            for c in range(2):
                pl.semaphore_signal(
                    barrier, inc=1, device_id=(me - d, base + c), device_id_type=MESH
                )

        @pl.when(me + d < n_ctx)
        def _():
            for c in range(2):
                pl.semaphore_signal(
                    barrier, inc=1, device_id=(me + d, base + c), device_id_type=MESH
                )

        expected = expected + jnp.where(me >= d, 2, 0) + jnp.where(me + d < n_ctx, 2, 0)

    dqt[...] = jnp.zeros_like(dqt)
    g[0] = jnp.zeros(g.shape[1:], g.dtype)
    g[SPAN] = jnp.zeros(g.shape[1:], g.dtype)

    places = [
        me * rows + i * part + lax.broadcasted_iota(jnp.int32, (1, part), 1) for i in range(2)
    ]

    def one_doc(j, carry):
        end, a, b = carry
        end = end + doc_ref[j]
        return end, jnp.where(places[0] >= end, end, a), jnp.where(places[1] >= end, end, b)

    none = jnp.zeros((1, part), jnp.int32)
    _, st[0], st[1] = lax.fori_loop(0, doc_ref.shape[0], one_doc, (jnp.int32(0), none, none))

    for c in loads:
        c.wait()
    hb[0, core] = kv[core]

    def turn(slot):
        for i in range(2):
            for h in range(heads):
                cols = slice(h * dim, (h + 1) * dim)
                qt[slot, h, i] = q[slot, i, :, cols].T
                dot[slot, h, i] = do[slot, i, :, cols].T

    turn(0)
    for i in range(2):
        for h in range(heads):
            cols = slice(h * dim, (h + 1) * dim)
            dl[0, i, h : h + 1, :] = jnp.sum(
                dot[0, h, i].astype(jnp.float32) * o[i, :, cols].T.astype(jnp.float32),
                axis=0,
                keepdims=True,
            )

    pl.semaphore_wait(barrier, expected)

    def remote(src, dst, send, recv, ctx, dev):
        return pltpu.make_async_remote_copy(
            src, dst, send, recv, device_id=(ctx, dev), device_id_type=MESH
        )

    swaps = [
        remote(s, d, ps_sem.at[n], pr_sem.at[n], me, pair)
        for n, (s, d) in enumerate(
            (
                (kv.at[1 - core], hb.at[0, core]),
                (q.at[0], q.at[1]),
                (do.at[0], do.at[1]),
                (ln.at[0], ln.at[1]),
                (dl.at[0], dl.at[1]),
                (g.at[0, 1 - core], r0),
            )
        )
    ]

    def ahead(d, c):
        return remote(
            kv.at[c], hb.at[d, core], hs_sem.at[d - 1, c], hr_sem.at[d - 1, core],
            me + d, base + c,
        )

    def arrived(d, s):
        return remote(
            kv.at[0], hb.at[d, s], hs_sem.at[d - 1, 0], hr_sem.at[d - 1, s], me, pair
        )

    def back(d, c):
        return remote(
            sb.at[d - 1, c], rb.at[d - 1, core], gs_sem.at[d - 1, c], gr_sem.at[d - 1, core],
            me - d, base + c,
        )

    def returned(d, s):
        return remote(
            sb.at[d - 1, 0], rb.at[d - 1, s], gs_sem.at[d - 1, 0], gr_sem.at[d - 1, s], me, pair
        )

    def hand(h):
        return remote(dqt.at[1, h], dqi.at[h], qs_sem.at[h], qr_sem.at[h], me, pair)

    swaps[0].start()
    for d in GATHER:

        @pl.when(me + d < n_ctx)
        def _():
            for c in range(2):
                ahead(d, c).start()

    for c in swaps[1:5]:
        c.start()

    def await_block(d):
        @pl.when(me >= d)
        def _():
            for s in range(2):
                arrived(d, s).wait_recv()

        @pl.when(me < d)
        def _():
            hb[d] = jnp.zeros(hb.shape[1:], hb.dtype)

    def take(d):
        kt[...] = jnp.concatenate([hb[d, 0, :half], hb[d, 1, :half]], axis=0)
        kn[...] = kt[...].T
        vn[...] = jnp.concatenate([hb[d, 0, half:], hb[d, 1, half:]], axis=0).T

    krow = lax.broadcasted_iota(jnp.int32, (part, part), 0)
    qcol = lax.broadcasted_iota(jnp.int32, (part, part), 1)

    def one_head(d, slot, h, halves, causal, fresh):
        cols = slice(h * dim, (h + 1) * dim)
        first = (me - d) * rows + core * part
        total = None
        for i in halves:
            s = mm(kn[...], q[slot, i, :, cols], NT)
            dp = mm(vn[...], do[slot, i, :, cols], NT)
            allowed = krow >= st[i] - first
            if causal:
                allowed = allowed & (krow <= qcol)
            p = jnp.where(
                allowed,
                jnp.exp2(s * (scale * LOG2E) - ln[slot, i, h : h + 1, :] * LOG2E),
                0.0,
            )
            ds = p * (dp - dl[slot, i, h : h + 1, :])
            pb = p.astype(jnp.bfloat16)
            dsb = ds.astype(jnp.bfloat16)
            gk = mm(qt[slot, h, i], dsb, NT)
            gv = mm(dot[slot, h, i], pb, NT)
            total = (gk, gv) if total is None else (total[0] + gk, total[1] + gv)
            dqt[slot, h, i] += mm(kt[...], dsb, NN)
        gk, gv = total
        for c in range(2):
            dims = slice(c * half, (c + 1) * half)
            if fresh:
                g[d, c, 0:half] = gk[dims]
                g[d, c, half:dim] = gv[dims]
            else:
                g[d, c, 0:half] += gk[dims]
                g[d, c, half:dim] += gv[dims]

    def give(d):
        @pl.when(me >= d)
        def _():
            for c in range(2):
                back(d, c).start()

    swaps[0].wait_recv()
    take(0)
    for h in range(heads):
        one_head(0, 0, h, (core,), True, False)
    for c in swaps[1:5]:
        c.wait_recv()
    turn(1)
    for h in range(heads):
        one_head(0, 1, h, (core,), True, False)

    await_block(SPAN)
    side = SPAN * core
    take(side)
    for slot in range(2):
        for h in range(heads):
            one_head(side, slot, h, (1 - core,), False, False)
    swaps[5].start()

    pending = None
    for d in BLOCKS:
        await_block(d)
        take(d)
        if pending is not None:
            give(pending)
        for slot in range(2):
            for h in range(heads):
                one_head(d, slot, h, (0, 1), False, slot == 0 and h == 0)
        sb[d - 1] = g[d].astype(jnp.bfloat16)
        pending = d

    take(SPAN)
    give(pending)
    for h in range(heads):
        one_head(SPAN, 1, h, (core,), False, False)
        if h:
            hand(h - 1).start()
    for h in range(heads):
        one_head(SPAN, 0, h, (core,), False, False)
        if h == 0:
            hand(heads - 1).start()
    sb[SPAN - 1] = g[SPAN].astype(jnp.bfloat16)

    stores = []
    for i in range(2):
        at = pl.ds(i * part, part)
        stores += [(dq.at[i], dq_hbm.at[at]), (dk.at[i], dk_hbm.at[:, at]), (dv.at[i], dv_hbm.at[:, at])]
    stores = [pltpu.make_async_copy(s, d, out_sem.at[n]) for n, (s, d) in enumerate(stores)]

    for h in range(heads):
        hand(h).wait_recv()
        if h == 0:
            give(SPAN)
        for i in range(2):
            dq[i, :, h * dim : (h + 1) * dim] = (
                (dqt[0, h, i] + dqi[h, i]).T * scale
            ).astype(jnp.bfloat16)
    stores[0].start()
    stores[3].start()

    swaps[5].wait_recv()
    sums = [g[0, core], r0[...]]
    for d in RETURN:

        @pl.when(me + d < n_ctx)
        def _():
            for s in range(2):
                returned(d, s).wait_recv()

        @pl.when(me + d >= n_ctx)
        def _():
            rb[d - 1] = jnp.zeros(rb.shape[1:], rb.dtype)

        sums[0] = sums[0] + rb[d - 1, core].astype(jnp.float32)
        sums[1] = sums[1] + rb[d - 1, 1 - core].astype(jnp.float32)
    for i, total in ((core, sums[0]), (1 - core, sums[1])):
        dk[i] = (total[:half] * scale).astype(jnp.bfloat16)
        dv[i] = total[half:].astype(jnp.bfloat16)
    for n in (1, 2, 4, 5):
        stores[n].start()

    for c in swaps:
        c.wait_send()
    for h in range(heads):
        hand(h).wait_send()
    for d in range(1, SPAN + 1):

        @pl.when(me + d < n_ctx)
        def _():
            for c in range(2):
                ahead(d, c).wait_send()

        @pl.when(me >= d)
        def _():
            for c in range(2):
                back(d, c).wait_send()

    for c in stores:
        c.wait()


def local(queries, key_states, value_states, attn_out, grad_out, log_norm, doc_lengths):
    rows, half = key_states.shape
    dim = 2 * half
    part = rows // 2
    heads = queries.shape[1] // dim
    wide = heads * dim
    bf, f32 = jnp.bfloat16, jnp.float32
    blocks = SPAN + 1
    anywhere = pl.BlockSpec(memory_space=pl.ANY)
    vmem, dma = pltpu.VMEM, pltpu.SemaphoreType.DMA
    grad_q, grad_k, grad_v = pl.pallas_call(
        kernel,
        out_shape=(
            jax.ShapeDtypeStruct((rows, wide), bf),
            jax.ShapeDtypeStruct((half, rows), bf),
            jax.ShapeDtypeStruct((half, rows), bf),
        ),
        in_specs=[pl.BlockSpec(memory_space=pltpu.SMEM)] + [anywhere] * 6,
        out_specs=(anywhere,) * 3,
        scratch_shapes=[
            vmem((2, dim, part), bf),
            vmem((2, 2, part, wide), bf),
            vmem((2, 2, part, wide), bf),
            vmem((2, part, wide), bf),
            vmem((2, heads, 2, dim, part), bf),
            vmem((2, heads, 2, dim, part), bf),
            vmem((2, 2, heads, part), f32),
            vmem((2, 2, heads, part), f32),
            vmem((2, 1, part), jnp.int32),
            vmem((blocks, 2, dim, part), bf),
            vmem((part, dim), bf),
            vmem((part, dim), bf),
            vmem((dim, part), bf),
            vmem((blocks, 2, dim, part), f32),
            vmem((dim, part), f32),
            vmem((SPAN, 2, dim, part), bf),
            vmem((SPAN, 2, dim, part), bf),
            vmem((2, heads, 2, dim, part), f32),
            vmem((heads, 2, dim, part), f32),
            vmem((2, part, wide), bf),
            vmem((2, half, part), bf),
            vmem((2, half, part), bf),
            dma((12,)), dma((6,)), dma((6,)), dma((6,)),
            dma((SPAN, 2)), dma((SPAN, 2)), dma((SPAN, 2)), dma((SPAN, 2)),
            dma((heads,)), dma((heads,)),
        ],
        compiler_params=pltpu.CompilerParams(
            collective_id=0, has_side_effects=True, vmem_limit_bytes=60 * 2**20
        ),
    )(doc_lengths, queries, key_states.T, value_states.T, attn_out, grad_out, log_norm)
    return grad_q, grad_k.T, grad_v.T


def solution(mesh):
    in_specs = (
        P("ctx", "head"), P("ctx", "head"), P("ctx", "head"), P("ctx", "head"),
        P("ctx", "head"), P("head", "ctx"), P(),
    )
    out_specs = (P("ctx", "head"), P("ctx", "head"), P("ctx", "head"))
    return jax.shard_map(local, mesh=mesh, in_specs=in_specs, out_specs=out_specs, check_vma=False)
```

time: 43.5 us -> 44.8 us (1.030)
  the two profiles are of different devices: /device:TPU:1 before, /device:TPU:113 now
where the time goes in v2:
time: 44.8 us; the launch traced here: 44.6 us
  Pallas kernels  40.5 us (90%)
  local copies, waits for them, and re-layouts  3.4 us (8%)
  between operations  0.65 us (1%)
    pallas_call x1, Pallas kernels, local(): pl.pallas_call(kernel, out_shape=(jax.ShapeDtypeStruct((rows, wide), bf),...  40.5 us
    unnamed x7, local copies, waits for them, and re-layouts  3.4 us

profile of v2, /device:TPU:113, one launch (start us, length us, event | category | flops | bytes accessed | tf_op | source)
XLA Modules:
  0.0 44.6 jit_solution(15781452480191602447)
XLA Ops:
  0.6 40.5 %shard_map.94 = (bf16[512,512]{1,0:T(8,128)(2,1)}, bf16[64,512]{1,0:T(8,128)(2,1)}, bf16[64,512]{1,0:T(8,128)(2,1)}) custom-call(s32[64]{0:T(128)} %doc_ref.1, bf16[512,512]{1,0:T(8,128)(2,1)} %q_hbm.1, bf16[64,512]{1,0:T(8,128)(2,1)} %bitcast.4, bf16[64,512]{1,0:T(8,128)(2,1)} %bitcast.5, bf16[512,512]{1,0:T(8,128)(2,1)} %o_hbm.1, bf16[512,512]{1,0:T(8,128)(2,1)} %do_hbm.1, ...), custom_call_target="tpu_custom_call" | custom-call | tf_op jit(solution)/shard_map/pallas_call | solution.py:337
  41.2 0.0 copy-start.1
  41.2 1.9 %copy.13 = bf16[512,512]{1,0:T(8,128)(2,1)} copy(bf16[512,512]{1,0:T(8,128)(2,1)} %get-tuple-element.12) | data formatting | bytes 1048576
  43.1 0.0 copy-done.1
  43.1 0.0 copy-start
  43.1 0.6 %copy.14 = bf16[512,64]{0,1:T(8,128)(2,1)} copy(bf16[512,64]{0,1:T(8,128)(2,1)S(1)} %bitcast.7) | data formatting | bytes 131072
  43.7 0.2 copy-done
  43.9 0.6 %copy.15 = bf16[512,64]{0,1:T(8,128)(2,1)} copy(bf16[512,64]{0,1:T(8,128)(2,1)S(1)} %bitcast.6) | data formatting | bytes 131072
Async XLA Ops:
  41.2 1.9 %copy-start.1 = (bf16[64,512]{1,0:T(8,128)(2,1)S(1)}, bf16[64,512]{1,0:T(8,128)(2,1)}, u32[]{:S(2)}) copy-start(bf16[64,512]{1,0:T(8,128)(2,1)} %get-tuple-element.7) | copy-start | bytes 196612
  43.1 0.9 %copy-start = (bf16[64,512]{1,0:T(8,128)(2,1)S(1)}, bf16[64,512]{1,0:T(8,128)(2,1)}, u32[]{:S(2)}) copy-start(bf16[64,512]{1,0:T(8,128)(2,1)} %get-tuple-element.8) | copy-start | bytes 196612

commit v3 on v2

--- a/solution.py
+++ b/solution.py
@@ -10,9 +10,10 @@
 NT = (((1,), (1,)), ((), ()))
 NN = (((1,), (0,)), ((), ()))
 SPAN = 4
-GATHER = (4, 1, 2, 3)
+GATHER = (4, 1, 3, 2)
 BLOCKS = (1, 2, 3)
 RETURN = (1, 2, 3, 4)
+RELAY = (2, 3)
 
 
 def mm(a, b, dims):
@@ -22,19 +23,20 @@
 def kernel(
     doc_ref, q_hbm, k_hbm, v_hbm, o_hbm, do_hbm, ln_hbm,
     dq_hbm, dk_hbm, dv_hbm,
-    kv, q, do, o, qt, dot, ln, dl, st, hb, kn, vn, kt, g, r0, sb, rb, dqt, dqi, dq, dk, dv,
-    in_sem, out_sem, ps_sem, pr_sem, hs_sem, hr_sem, gs_sem, gr_sem, qs_sem, qr_sem,
+    kv, q, do, o, ln, dl, st, hb, kn, vn, kt, pb, dsb, g, g0, r0, sb, rb, dqt, dqi, dq, dk, dv,
+    in_sem, out_sem, ps_sem, pr_sem, hs_sem, hr_sem, gs_sem, gr_sem, qs_sem, qr_sem, re_sem,
 ):
     part = q.shape[2]
     rows = 2 * part
-    heads = qt.shape[1]
-    dim = qt.shape[3]
+    heads = dqt.shape[1]
+    dim = dqt.shape[3]
     half = dim // 2
     n_ctx = lax.axis_size("ctx")
     scale = dim ** (-0.5)
     me = lax.axis_index("ctx")
     head = lax.axis_index("head")
     core = lax.rem(head, 2)
+    ring = lax.rem(me, SPAN)
     base = head - core
     pair = base + 1 - core
 
@@ -94,22 +96,11 @@
         c.wait()
     hb[0, core] = kv[core]
 
-    def turn(slot):
-        for i in range(2):
-            for h in range(heads):
-                cols = slice(h * dim, (h + 1) * dim)
-                qt[slot, h, i] = q[slot, i, :, cols].T
-                dot[slot, h, i] = do[slot, i, :, cols].T
-
-    turn(0)
     for i in range(2):
         for h in range(heads):
             cols = slice(h * dim, (h + 1) * dim)
-            dl[0, i, h : h + 1, :] = jnp.sum(
-                dot[0, h, i].astype(jnp.float32) * o[i, :, cols].T.astype(jnp.float32),
-                axis=0,
-                keepdims=True,
-            )
+            prod = do[0, i, :, cols].astype(jnp.float32) * o[i, :, cols].astype(jnp.float32)
+            dl[0, i, h : h + 1, :] = jnp.sum(prod.T, axis=0, keepdims=True)
 
     pl.semaphore_wait(barrier, expected)
 
@@ -127,7 +118,7 @@
                 (do.at[0], do.at[1]),
                 (ln.at[0], ln.at[1]),
                 (dl.at[0], dl.at[1]),
-                (g.at[0, 1 - core], r0),
+                (g0.at[1 - core], r0),
             )
         )
     ]
@@ -143,6 +134,16 @@
             kv.at[0], hb.at[d, s], hs_sem.at[d - 1, 0], hr_sem.at[d - 1, s], me, pair
         )
 
+    def sends(d):
+        near = me + d < n_ctx
+        return near & (ring + d < SPAN) if d in RELAY else near
+
+    def onward(d, s):
+        return remote(
+            hb.at[SPAN, s], hb.at[d, s], re_sem.at[d - RELAY[0], s], hr_sem.at[d - 1, s],
+            me + d - SPAN, head,
+        )
+
     def back(d, c):
         return remote(
             sb.at[d - 1, c], rb.at[d - 1, core], gs_sem.at[d - 1, c], gr_sem.at[d - 1, core],
@@ -160,7 +161,7 @@
     swaps[0].start()
     for d in GATHER:
 
-        @pl.when(me + d < n_ctx)
+        @pl.when(sends(d))
         def _():
             for c in range(2):
                 ahead(d, c).start()
@@ -186,37 +187,39 @@
     krow = lax.broadcasted_iota(jnp.int32, (part, part), 0)
     qcol = lax.broadcasted_iota(jnp.int32, (part, part), 1)
 
-    def one_head(d, slot, h, halves, causal, fresh):
-        cols = slice(h * dim, (h + 1) * dim)
+    def attend(d, slot, halves, causal, fresh, between=None):
         first = (me - d) * rows + core * part
-        total = None
-        for i in halves:
-            s = mm(kn[...], q[slot, i, :, cols], NT)
-            dp = mm(vn[...], do[slot, i, :, cols], NT)
-            allowed = krow >= st[i] - first
-            if causal:
-                allowed = allowed & (krow <= qcol)
-            p = jnp.where(
-                allowed,
-                jnp.exp2(s * (scale * LOG2E) - ln[slot, i, h : h + 1, :] * LOG2E),
-                0.0,
-            )
-            ds = p * (dp - dl[slot, i, h : h + 1, :])
-            pb = p.astype(jnp.bfloat16)
-            dsb = ds.astype(jnp.bfloat16)
-            gk = mm(qt[slot, h, i], dsb, NT)
-            gv = mm(dot[slot, h, i], pb, NT)
-            total = (gk, gv) if total is None else (total[0] + gk, total[1] + gv)
-            dqt[slot, h, i] += mm(kt[...], dsb, NN)
-        gk, gv = total
+        for h in range(heads):
+            cols = slice(h * dim, (h + 1) * dim)
+            for n, i in enumerate(halves):
+                s = mm(kn[...], q[slot, i, :, cols], NT)
+                dp = mm(vn[...], do[slot, i, :, cols], NT)
+                allowed = krow >= st[i] - first
+                if causal:
+                    allowed = allowed & (krow <= qcol)
+                p = jnp.where(
+                    allowed,
+                    jnp.exp2(s * (scale * LOG2E) - ln[slot, i, h : h + 1, :] * LOG2E),
+                    0.0,
+                )
+                pb[h, n] = p.astype(jnp.bfloat16)
+                dsb[h, n] = (p * (dp - dl[slot, i, h : h + 1, :])).astype(jnp.bfloat16)
+        if between is not None:
+            between()
+        gk, gv = (0.0, 0.0) if fresh else (g[d, 0], g[d, 1])
+        for h in range(heads):
+            cols = slice(h * dim, (h + 1) * dim)
+            for n, i in enumerate(halves):
+                gk = gk + mm(dsb[h, n], q[slot, i, :, cols], NN)
+                gv = gv + mm(pb[h, n], do[slot, i, :, cols], NN)
+                dqt[slot, h, i] += mm(kt[...], dsb[h, n], NN)
+        g[d, 0], g[d, 1] = gk, gv
+
+    def lay(dst, d):
+        gk, gv = g[d, 0].T, g[d, 1].T
         for c in range(2):
-            dims = slice(c * half, (c + 1) * half)
-            if fresh:
-                g[d, c, 0:half] = gk[dims]
-                g[d, c, half:dim] = gv[dims]
-            else:
-                g[d, c, 0:half] += gk[dims]
-                g[d, c, half:dim] += gv[dims]
+            dst[c, 0:half] = gk[c * half : (c + 1) * half].astype(dst.dtype)
+            dst[c, half:dim] = gv[c * half : (c + 1) * half].astype(dst.dtype)
 
     def give(d):
         @pl.when(me >= d)
@@ -226,45 +229,48 @@
 
     swaps[0].wait_recv()
     take(0)
-    for h in range(heads):
-        one_head(0, 0, h, (core,), True, False)
+    attend(0, 0, (core,), True, False)
     for c in swaps[1:5]:
         c.wait_recv()
-    turn(1)
-    for h in range(heads):
-        one_head(0, 1, h, (core,), True, False)
+    attend(0, 1, (core,), True, False)
 
     await_block(SPAN)
+    for d in RELAY:
+
+        @pl.when((ring + d >= SPAN) & (me >= SPAN))
+        def _():
+            for s in range(2):
+                onward(d, s).start()
+
     side = SPAN * core
     take(side)
     for slot in range(2):
-        for h in range(heads):
-            one_head(side, slot, h, (1 - core,), False, False)
-    swaps[5].start()
+        attend(side, slot, (1 - core,), False, False)
+    lay(g0, 0)
 
     pending = None
     for d in BLOCKS:
         await_block(d)
         take(d)
-        if pending is not None:
+        if pending is None:
+            swaps[5].start()
+        else:
             give(pending)
         for slot in range(2):
-            for h in range(heads):
-                one_head(d, slot, h, (0, 1), False, slot == 0 and h == 0)
-        sb[d - 1] = g[d].astype(jnp.bfloat16)
+            attend(d, slot, (0, 1), False, slot == 0)
+        lay(sb.at[d - 1], d)
         pending = d
 
     take(SPAN)
     give(pending)
-    for h in range(heads):
-        one_head(SPAN, 1, h, (core,), False, False)
-        if h:
-            hand(h - 1).start()
-    for h in range(heads):
-        one_head(SPAN, 0, h, (core,), False, False)
-        if h == 0:
-            hand(heads - 1).start()
-    sb[SPAN - 1] = g[SPAN].astype(jnp.bfloat16)
+    attend(SPAN, 1, (core,), False, False)
+
+    def hand_over():
+        for h in range(heads):
+            hand(h).start()
+
+    attend(SPAN, 0, (core,), False, False, hand_over)
+    lay(sb.at[SPAN - 1], SPAN)
 
     stores = []
     for i in range(2):
@@ -284,7 +290,7 @@
     stores[3].start()
 
     swaps[5].wait_recv()
-    sums = [g[0, core], r0[...]]
+    sums = [g0[core], r0[...]]
     for d in RETURN:
 
         @pl.when(me + d < n_ctx)
@@ -310,7 +316,7 @@
         hand(h).wait_send()
     for d in range(1, SPAN + 1):
 
-        @pl.when(me + d < n_ctx)
+        @pl.when(sends(d))
         def _():
             for c in range(2):
                 ahead(d, c).wait_send()
@@ -320,7 +326,25 @@
             for c in range(2):
                 back(d, c).wait_send()
 
+    for d in RELAY:
+
+        @pl.when((ring + d >= SPAN) & (me >= SPAN))
+        def _():
+            for s in range(2):
+                onward(d, s).wait_send()
+
     for c in stores:
+        c.wait()
+
+
+def finish(dq, dk, dv, dq_out, dk_out, dv_out, sem):
+    copies = [
+        pltpu.make_async_copy(s, d, sem.at[n])
+        for n, (s, d) in enumerate(((dq, dq_out), (dk, dk_out), (dv, dv_out)))
+    ]
+    for c in copies:
+        c.start()
+    for c in copies:
         c.wait()
 
 
@@ -348,8 +372,6 @@
             vmem((2, 2, part, wide), bf),
             vmem((2, 2, part, wide), bf),
             vmem((2, part, wide), bf),
-            vmem((2, heads, 2, dim, part), bf),
-            vmem((2, heads, 2, dim, part), bf),
             vmem((2, 2, heads, part), f32),
             vmem((2, 2, heads, part), f32),
             vmem((2, 1, part), jnp.int32),
@@ -357,7 +379,10 @@
             vmem((part, dim), bf),
             vmem((part, dim), bf),
             vmem((dim, part), bf),
-            vmem((blocks, 2, dim, part), f32),
+            vmem((heads, 2, part, part), bf),
+            vmem((heads, 2, part, part), bf),
+            vmem((blocks, 2, part, dim), f32),
+            vmem((2, dim, part), f32),
             vmem((dim, part), f32),
             vmem((SPAN, 2, dim, part), bf),
             vmem((SPAN, 2, dim, part), bf),
@@ -368,12 +393,24 @@
             vmem((2, half, part), bf),
             dma((12,)), dma((6,)), dma((6,)), dma((6,)),
             dma((SPAN, 2)), dma((SPAN, 2)), dma((SPAN, 2)), dma((SPAN, 2)),
-            dma((heads,)), dma((heads,)),
+            dma((heads,)), dma((heads,)), dma((2, 2)),
         ],
         compiler_params=pltpu.CompilerParams(
-            collective_id=0, has_side_effects=True, vmem_limit_bytes=60 * 2**20
+            collective_id=0, has_side_effects=True, vmem_limit_bytes=40 * 2**20
         ),
     )(doc_lengths, queries, key_states.T, value_states.T, attn_out, grad_out, log_norm)
+    grad_q, grad_k, grad_v = pl.pallas_call(
+        finish,
+        out_shape=(
+            jax.ShapeDtypeStruct((rows, wide), bf),
+            jax.ShapeDtypeStruct((half, rows), bf),
+            jax.ShapeDtypeStruct((half, rows), bf),
+        ),
+        in_specs=[pl.BlockSpec(memory_space=vmem)] * 3,
+        out_specs=(anywhere,) * 3,
+        scratch_shapes=[dma((3,))],
+        compiler_params=pltpu.CompilerParams(vmem_limit_bytes=2 * 2**20),
+    )(grad_q, grad_k, grad_v)
     return grad_q, grad_k.T, grad_v.T
 
 

time: 44.8 us -> 44 us (0.982)
  Pallas kernels: 40.5 us -> 36.7 us
  local copies, waits for them, and re-layouts: 3.4 us -> 6.15 us
    pallas_call x1, Pallas kernels: 40.5 us -> 35.9 us  [local(): pl.pallas_call(kernel, out_shape=(jax.ShapeDtypeStruct((rows, wide), bf),...]
    unnamed x7 -> x14, local copies, waits for them, and re-layouts: 3.4 us -> 6.15 us
    pallas_call x0 -> x1, Pallas kernels: none -> 0.85 us  [local(): pl.pallas_call(finish, out_shape=(jax.ShapeDtypeStruct((rows, wide), bf),...]
where the time goes in v3:
time: 44 us; the launch traced here: 43.7 us
  Pallas kernels  36.7 us (83%)
  local copies, waits for them, and re-layouts  6.15 us (14%)
  between operations  0.82 us (2%)
    pallas_call x1, Pallas kernels, local(): pl.pallas_call(kernel, out_shape=(jax.ShapeDtypeStruct((rows, wide), bf),...  35.9 us
    unnamed x14, local copies, waits for them, and re-layouts  6.15 us

profile of v3, /device:TPU:113, one launch (start us, length us, event | category | flops | bytes accessed | tf_op | source)
XLA Modules:
  0.0 43.7 jit_solution(4108282396489481277)
XLA Ops:
  0.6 0.0 copy-start.6
  0.6 0.6 %copy-done.6 = s32[64]{0:T(128)S(1)} copy-done((s32[64]{0:T(128)S(1)}, s32[64]{0:T(128)}, u32[]{:S(2)}) %copy-start.6) | copy-done | bytes 280
  1.3 0.0 copy-start
  1.3 1.0 %copy-done = bf16[512,512]{1,0:T(8,128)(2,1)S(1)} copy-done((bf16[512,512]{1,0:T(8,128)(2,1)S(1)}, bf16[512,512]{1,0:T(8,128)(2,1)}, u32[]{:S(2)}) %copy-start) | copy-done | bytes 524312
  2.3 0.0 copy-start.1
  2.3 1.0 %copy-done.1 = bf16[512,512]{1,0:T(8,128)(2,1)S(1)} copy-done((bf16[512,512]{1,0:T(8,128)(2,1)S(1)}, bf16[512,512]{1,0:T(8,128)(2,1)}, u32[]{:S(2)}) %copy-start.1) | copy-done | bytes 524312
  3.4 0.0 copy-start.2
  3.4 1.0 %copy-done.2 = bf16[512,512]{1,0:T(8,128)(2,1)S(1)} copy-done((bf16[512,512]{1,0:T(8,128)(2,1)S(1)}, bf16[512,512]{1,0:T(8,128)(2,1)}, u32[]{:S(2)}) %copy-start.2) | copy-done | bytes 524312
  4.4 0.0 copy-start.3
  4.4 0.8 %copy-done.3 = bf16[512,64]{0,1:T(8,128)(2,1)S(1)} copy-done((bf16[512,64]{0,1:T(8,128)(2,1)S(1)}, bf16[512,64]{0,1:T(8,128)(2,1)}, u32[]{:S(2)}) %copy-start.3) | copy-done | bytes 65560
  5.3 0.0 copy-start.4
  5.3 0.8 %copy-done.4 = bf16[512,64]{0,1:T(8,128)(2,1)S(1)} copy-done((bf16[512,64]{0,1:T(8,128)(2,1)S(1)}, bf16[512,64]{0,1:T(8,128)(2,1)}, u32[]{:S(2)}) %copy-start.4) | copy-done | bytes 65560
  6.1 0.0 copy-start.5
  6.1 0.7 %copy-done.5 = f32[4,512]{1,0:T(4,128)S(1)} copy-done((f32[4,512]{1,0:T(4,128)S(1)}, f32[4,512]{1,0:T(4,128)}, u32[]{:S(2)}) %copy-start.5) | copy-done | bytes 8216
  6.8 35.9 %shard_map.94 = (bf16[512,512]{1,0:T(8,128)(2,1)S(1)}, bf16[64,512]{1,0:T(8,128)(2,1)S(1)}, bf16[64,512]{1,0:T(8,128)(2,1)S(1)}) custom-call(s32[64]{0:T(128)S(1)} %copy-done.6, bf16[512,512]{1,0:T(8,128)(2,1)S(1)} %copy-done, bf16[64,512]{1,0:T(8,128)(2,1)S(1)} %bitcast.4, bf16[64,512]{1,0:T(8,128)(2,1)S(1)} %bitcast.5, bf16[512,512]{1,0:T(8,128)(2,1)S(1)} %copy-done.1, ...), custom_call_target="tpu_custom_call" | custom-call | tf_op jit(solution)/shard_map/pallas_call | solution.py:361
  42.7 0.9 %shard_map.95 = (bf16[512,512]{1,0:T(8,128)(2,1)}, bf16[64,512]{1,0:T(8,128)(2,1)}, bf16[64,512]{1,0:T(8,128)(2,1)}) custom-call(bf16[512,512]{1,0:T(8,128)(2,1)S(1)} %get-tuple-element.9.dq, bf16[64,512]{1,0:T(8,128)(2,1)S(1)} %get-tuple-element.10.dk, bf16[64,512]{1,0:T(8,128)(2,1)S(1)} %get-tuple-element.11.dv), custom_call_target="tpu_custom_call" | custom-call | tf_op jit(solution)/shard_map/pallas_call | solution.py:402
Async XLA Ops:
  0.6 0.7 %copy-start.6 = (s32[64]{0:T(128)S(1)}, s32[64]{0:T(128)}, u32[]{:S(2)}) copy-start(s32[64]{0:T(128)} %doc_ref.1) | copy-start | bytes 772
  1.3 1.0 %copy-start = (bf16[512,512]{1,0:T(8,128)(2,1)S(1)}, bf16[512,512]{1,0:T(8,128)(2,1)}, u32[]{:S(2)}) copy-start(bf16[512,512]{1,0:T(8,128)(2,1)} %q_hbm.1) | copy-start | bytes 1572868
  2.3 1.0 %copy-start.1 = (bf16[512,512]{1,0:T(8,128)(2,1)S(1)}, bf16[512,512]{1,0:T(8,128)(2,1)}, u32[]{:S(2)}) copy-start(bf16[512,512]{1,0:T(8,128)(2,1)} %o_hbm.1) | copy-start | bytes 1572868
  3.4 1.0 %copy-start.2 = (bf16[512,512]{1,0:T(8,128)(2,1)S(1)}, bf16[512,512]{1,0:T(8,128)(2,1)}, u32[]{:S(2)}) copy-start(bf16[512,512]{1,0:T(8,128)(2,1)} %do_hbm.1) | copy-start | bytes 1572868
  4.4 0.8 %copy-start.3 = (bf16[512,64]{0,1:T(8,128)(2,1)S(1)}, bf16[512,64]{0,1:T(8,128)(2,1)}, u32[]{:S(2)}) copy-start(bf16[512,64]{0,1:T(8,128)(2,1)} %param.8) | copy-start | bytes 196612
  5.3 0.8 %copy-start.4 = (bf16[512,64]{0,1:T(8,128)(2,1)S(1)}, bf16[512,64]{0,1:T(8,128)(2,1)}, u32[]{:S(2)}) copy-start(bf16[512,64]{0,1:T(8,128)(2,1)} %param.9) | copy-start | bytes 196612
  6.1 0.7 %copy-start.5 = (f32[4,512]{1,0:T(4,128)S(1)}, f32[4,512]{1,0:T(4,128)}, u32[]{:S(2)}) copy-start(f32[4,512]{1,0:T(4,128)} %ln_hbm.1) | copy-start | bytes 24580

commit v4 on v3

--- a/solution.py
+++ b/solution.py
@@ -11,8 +11,8 @@
 NN = (((1,), (0,)), ((), ()))
 SPAN = 4
 GATHER = (4, 1, 3, 2)
-BLOCKS = (1, 2, 3)
-RETURN = (1, 2, 3, 4)
+BLOCKS = (1, 3, 2)
+RETURN = (1, 3, 2, 4)
 RELAY = (2, 3)
 
 
@@ -337,14 +337,20 @@
         c.wait()
 
 
-def finish(dq, dk, dv, dq_out, dk_out, dv_out, sem):
-    copies = [
-        pltpu.make_async_copy(s, d, sem.at[n])
-        for n, (s, d) in enumerate(((dq, dq_out), (dk, dk_out), (dv, dv_out)))
-    ]
-    for c in copies:
+def finish(dq, dk, dv, dq_out, dk_out, dv_out, q_buf, k_buf, v_buf, in_sem, out_sem):
+    size = q_buf.shape[0] // 4
+    hops = [(dk, k_buf, dk_out), (dv, v_buf, dv_out)]
+    for n in range(4):
+        at = pl.ds(n * size, size)
+        hops.append((dq.at[at], q_buf.at[at], dq_out.at[at]))
+    loads = [pltpu.make_async_copy(a, b, in_sem.at[n]) for n, (a, b, _) in enumerate(hops)]
+    stores = [pltpu.make_async_copy(b, c, out_sem.at[n]) for n, (_, b, c) in enumerate(hops)]
+    for c in loads:
         c.start()
-    for c in copies:
+    for a, b in zip(loads, stores):
+        a.wait()
+        b.start()
+    for c in stores:
         c.wait()
 
 
@@ -396,7 +402,7 @@
             dma((heads,)), dma((heads,)), dma((2, 2)),
         ],
         compiler_params=pltpu.CompilerParams(
-            collective_id=0, has_side_effects=True, vmem_limit_bytes=40 * 2**20
+            collective_id=0, has_side_effects=True, vmem_limit_bytes=60 * 2**20
         ),
     )(doc_lengths, queries, key_states.T, value_states.T, attn_out, grad_out, log_norm)
     grad_q, grad_k, grad_v = pl.pallas_call(
@@ -406,10 +412,13 @@
             jax.ShapeDtypeStruct((half, rows), bf),
             jax.ShapeDtypeStruct((half, rows), bf),
         ),
-        in_specs=[pl.BlockSpec(memory_space=vmem)] * 3,
+        in_specs=[anywhere] * 3,
         out_specs=(anywhere,) * 3,
-        scratch_shapes=[dma((3,))],
-        compiler_params=pltpu.CompilerParams(vmem_limit_bytes=2 * 2**20),
+        scratch_shapes=[
+            vmem((rows, wide), bf), vmem((half, rows), bf), vmem((half, rows), bf),
+            dma((6,)), dma((6,)),
+        ],
+        compiler_params=pltpu.CompilerParams(vmem_limit_bytes=60 * 2**20),
     )(grad_q, grad_k, grad_v)
     return grad_q, grad_k.T, grad_v.T
 

time: 44 us -> 37.3 us (0.85)
  local copies, waits for them, and re-layouts: 6.15 us -> 0 us
    unnamed x14 -> x0, local copies, waits for them, and re-layouts: 6.15 us -> none
    pallas_call x1, Pallas kernels: 35.9 us -> 34.5 us  [local(): pl.pallas_call(kernel, out_shape=(jax.ShapeDtypeStruct((rows, wide), bf),...]
    pallas_call x1, Pallas kernels: 0.85 us -> 1.93 us  [local(): pl.pallas_call(finish, out_shape=(jax.ShapeDtypeStruct((rows, wide), bf),...]
where the time goes in v4:
time: 37.3 us; the launch traced here: 37.2 us
  Pallas kernels  36.4 us (98%)
  between operations  0.8 us (2%)
    pallas_call x1, Pallas kernels, local(): pl.pallas_call(kernel, out_shape=(jax.ShapeDtypeStruct((rows, wide), bf),...  34.5 us
    pallas_call x1, Pallas kernels, local(): pl.pallas_call(finish, out_shape=(jax.ShapeDtypeStruct((rows, wide), bf),...  1.93 us

profile of v4, /device:TPU:113, one launch (start us, length us, event | category | flops | bytes accessed | tf_op | source)
XLA Modules:
  0.0 37.2 jit_solution(16793064440376583086)
XLA Ops:
  0.6 34.5 %shard_map.94 = (bf16[512,512]{1,0:T(8,128)(2,1)}, bf16[64,512]{1,0:T(8,128)(2,1)}, bf16[64,512]{1,0:T(8,128)(2,1)}) custom-call(s32[64]{0:T(128)} %doc_ref.1, bf16[512,512]{1,0:T(8,128)(2,1)} %q_hbm.1, bf16[64,512]{1,0:T(8,128)(2,1)} %bitcast.4, bf16[64,512]{1,0:T(8,128)(2,1)} %bitcast.5, bf16[512,512]{1,0:T(8,128)(2,1)} %o_hbm.1, bf16[512,512]{1,0:T(8,128)(2,1)} %do_hbm.1, ...), custom_call_target="tpu_custom_call" | custom-call | tf_op jit(solution)/shard_map/pallas_call | solution.py:367
  35.1 1.9 %shard_map.95 = (bf16[512,512]{1,0:T(8,128)(2,1)}, bf16[64,512]{1,0:T(8,128)(2,1)}, bf16[64,512]{1,0:T(8,128)(2,1)}) custom-call(bf16[512,512]{1,0:T(8,128)(2,1)} %get-tuple-element.9.dq, bf16[64,512]{1,0:T(8,128)(2,1)} %get-tuple-element.10.dk, bf16[64,512]{1,0:T(8,128)(2,1)} %get-tuple-element.11.dv), custom_call_target="tpu_custom_call" | custom-call | tf_op jit(solution)/shard_map/pallas_call | solution.py:408

commit v5 on v4

--- a/solution.py
+++ b/solution.py
@@ -272,6 +272,9 @@
     attend(SPAN, 0, (core,), False, False, hand_over)
     lay(sb.at[SPAN - 1], SPAN)
 
+    swaps[5].wait_recv()
+    give(SPAN)
+
     stores = []
     for i in range(2):
         at = pl.ds(i * part, part)
@@ -280,8 +283,6 @@
 
     for h in range(heads):
         hand(h).wait_recv()
-        if h == 0:
-            give(SPAN)
         for i in range(2):
             dq[i, :, h * dim : (h + 1) * dim] = (
                 (dqt[0, h, i] + dqi[h, i]).T * scale
@@ -289,7 +290,6 @@
     stores[0].start()
     stores[3].start()
 
-    swaps[5].wait_recv()
     sums = [g0[core], r0[...]]
     for d in RETURN:
 

time: 37.3 us -> 37.3 us (level)
  no operation moved by 1% of the time
where the time goes in v5:
time: 37.3 us; the launch traced here: 37.2 us
  Pallas kernels  36.4 us (98%)
  between operations  0.8 us (2%)
    pallas_call x1, Pallas kernels, local(): pl.pallas_call(kernel, out_shape=(jax.ShapeDtypeStruct((rows, wide), bf),...  34.5 us
    pallas_call x1, Pallas kernels, local(): pl.pallas_call(finish, out_shape=(jax.ShapeDtypeStruct((rows, wide), bf),...  1.93 us

profile of v5, /device:TPU:113, one launch (start us, length us, event | category | flops | bytes accessed | tf_op | source)
XLA Modules:
  0.0 37.2 jit_solution(16293835346201580607)
XLA Ops:
  0.6 34.5 %shard_map.94 = (bf16[512,512]{1,0:T(8,128)(2,1)}, bf16[64,512]{1,0:T(8,128)(2,1)}, bf16[64,512]{1,0:T(8,128)(2,1)}) custom-call(s32[64]{0:T(128)} %doc_ref.1, bf16[512,512]{1,0:T(8,128)(2,1)} %q_hbm.1, bf16[64,512]{1,0:T(8,128)(2,1)} %bitcast.4, bf16[64,512]{1,0:T(8,128)(2,1)} %bitcast.5, bf16[512,512]{1,0:T(8,128)(2,1)} %o_hbm.1, bf16[512,512]{1,0:T(8,128)(2,1)} %do_hbm.1, ...), custom_call_target="tpu_custom_call" | custom-call | tf_op jit(solution)/shard_map/pallas_call | solution.py:367
  35.1 1.9 %shard_map.95 = (bf16[512,512]{1,0:T(8,128)(2,1)}, bf16[64,512]{1,0:T(8,128)(2,1)}, bf16[64,512]{1,0:T(8,128)(2,1)}) custom-call(bf16[512,512]{1,0:T(8,128)(2,1)} %get-tuple-element.9.dq, bf16[64,512]{1,0:T(8,128)(2,1)} %get-tuple-element.10.dk, bf16[64,512]{1,0:T(8,128)(2,1)} %get-tuple-element.11.dv), custom_call_target="tpu_custom_call" | custom-call | tf_op jit(solution)/shard_map/pallas_call | solution.py:408

commit v6 on v5

--- a/solution.py
+++ b/solution.py
@@ -12,7 +12,7 @@
 SPAN = 4
 GATHER = (4, 1, 3, 2)
 BLOCKS = (1, 3, 2)
-RETURN = (1, 3, 2, 4)
+RETURN = (4, 1, 3, 2)
 RELAY = (2, 3)
 
 
@@ -248,32 +248,27 @@
         attend(side, slot, (1 - core,), False, False)
     lay(g0, 0)
 
-    pending = None
+    take(SPAN)
+    swaps[5].start()
+    for slot in range(2):
+        attend(SPAN, slot, (core,), False, False)
+    lay(sb.at[SPAN - 1], SPAN)
+
+    def hand_over():
+        for h in range(heads):
+            hand(h).start()
+
+    pending = SPAN
     for d in BLOCKS:
         await_block(d)
         take(d)
-        if pending is None:
-            swaps[5].start()
-        else:
-            give(pending)
-        for slot in range(2):
-            attend(d, slot, (0, 1), False, slot == 0)
+        give(pending)
+        attend(d, 1, (0, 1), False, True)
+        attend(d, 0, (0, 1), False, False, hand_over if d == BLOCKS[-1] else None)
         lay(sb.at[d - 1], d)
         pending = d
-
-    take(SPAN)
+    swaps[5].wait_recv()
     give(pending)
-    attend(SPAN, 1, (core,), False, False)
-
-    def hand_over():
-        for h in range(heads):
-            hand(h).start()
-
-    attend(SPAN, 0, (core,), False, False, hand_over)
-    lay(sb.at[SPAN - 1], SPAN)
-
-    swaps[5].wait_recv()
-    give(SPAN)
 
     stores = []
     for i in range(2):

time: 37.3 us -> 35.5 us (0.952)
  Pallas kernels: 36.4 us -> 34.5 us
    pallas_call x1, Pallas kernels: 34.5 us -> 32.6 us  [local(): pl.pallas_call(kernel, out_shape=(jax.ShapeDtypeStruct((rows, wide), bf),...]
where the time goes in v6:
time: 35.5 us; the launch traced here: 35.3 us
  Pallas kernels  34.5 us (97%)
  between operations  0.8 us (2%)
    pallas_call x1, Pallas kernels, local(): pl.pallas_call(kernel, out_shape=(jax.ShapeDtypeStruct((rows, wide), bf),...  32.6 us
    pallas_call x1, Pallas kernels, local(): pl.pallas_call(finish, out_shape=(jax.ShapeDtypeStruct((rows, wide), bf),...  1.93 us

profile of v6, /device:TPU:113, one launch (start us, length us, event | category | flops | bytes accessed | tf_op | source)
XLA Modules:
  0.0 35.3 jit_solution(2744904596496046100)
XLA Ops:
  0.6 32.6 %shard_map.94 = (bf16[512,512]{1,0:T(8,128)(2,1)}, bf16[64,512]{1,0:T(8,128)(2,1)}, bf16[64,512]{1,0:T(8,128)(2,1)}) custom-call(s32[64]{0:T(128)} %doc_ref.1, bf16[512,512]{1,0:T(8,128)(2,1)} %q_hbm.1, bf16[64,512]{1,0:T(8,128)(2,1)} %bitcast.4, bf16[64,512]{1,0:T(8,128)(2,1)} %bitcast.5, bf16[512,512]{1,0:T(8,128)(2,1)} %o_hbm.1, bf16[512,512]{1,0:T(8,128)(2,1)} %do_hbm.1, ...), custom_call_target="tpu_custom_call" | custom-call | tf_op jit(solution)/shard_map/pallas_call | solution.py:362
  33.2 1.9 %shard_map.95 = (bf16[512,512]{1,0:T(8,128)(2,1)}, bf16[64,512]{1,0:T(8,128)(2,1)}, bf16[64,512]{1,0:T(8,128)(2,1)}) custom-call(bf16[512,512]{1,0:T(8,128)(2,1)} %get-tuple-element.9.dq, bf16[64,512]{1,0:T(8,128)(2,1)} %get-tuple-element.10.dk, bf16[64,512]{1,0:T(8,128)(2,1)} %get-tuple-element.11.dv), custom_call_target="tpu_custom_call" | custom-call | tf_op jit(solution)/shard_map/pallas_call | solution.py:403
